TPU v7x, 32 devices: a whole 2x2x4 slice. The times are simulated.
32 devices in a mesh: row: 16 (over z, y, x), col: 2 (over core).
Axes of the slice: x: 2, y: 2, z: 4, core: 2. Of those that a mesh axis runs over, the one named last changes fastest.
Arguments:
- blocks: float32 [16, 2, 40, 128, 128], P('row', 'col'), may hold values from -0.078125 to 0.078125
- block_rows: int32 [16, 2, 40], P('row', 'col'), may hold values from 0 to 15
- block_cols: int32 [16, 2, 40], P(None, 'col'), may hold values from 0 to 127, as said below
- start_basis: float32 [32, 32768], P(None, ('row', 'col')), may hold values from -6 to 6
- targets: int32 [16], replicated, may hold values from 0 to 31, as said below
Outputs:
- right_basis: float32 [32, 32768], P(None, ('row', 'col'))
- left_basis: float32 [32, 32768], P(None, ('row', 'col'))
- triangle: float32 [32, 32], replicated
Inputs may be any that keep to these rules, and one draw needn't show every extreme that they name: For every r, c and o < 16, all entries block_cols[r, c, n] with block_cols[r, c, n] // 8 = o are equal. `targets`: 16 distinct indices.
All inputs are finite; a program needn't handle non-finite values.
Results may differ from a plain program's by a relative error of at most 0.0001.
Values sent between devices are 32-bit elements; how exact they have to be, the bound alone decides.
No kernel may reach another device: no remote copies, remote signals or barrier semaphores. Data moves between devices by JAX's collectives and lax.ppermute only.
A program may use at most 64 MiB of HBM per device.

v0:
```python
import jax
import jax.numpy as jnp
from jax import lax
from jax.sharding import PartitionSpec as P

OUTER = 2
INNER = 4
highest = lax.Precision.HIGHEST


def lower_solve(lower, vectors):
    return lax.linalg.triangular_solve(lower, vectors, left_side=True, lower=True)


def gram_local(vectors):
    return jnp.dot(vectors, vectors.T, precision=highest)


def basis_factor(trial_basis, total_rows):
    gram_sum = lax.psum(gram_local(trial_basis), ("row", "col"))
    return jnp.linalg.cholesky(gram_sum / total_rows)


def multiply(vectors, block_tiles, tables):
    pick_hot, owners_mine, owner_hot, row_hot, rows_local = tables
    count_vectors = vectors.shape[0]
    block_size = block_tiles.shape[-1]
    segments = vectors.reshape(count_vectors, -1, block_size)
    outgoing = jnp.einsum("rt,ktb->rkb", pick_hot, segments, precision=highest)
    incoming = lax.all_to_all(outgoing, "row", split_axis=0, concat_axis=0, tiled=True)
    picked = incoming[owners_mine]
    products = jnp.einsum("nij,nkj->kni", block_tiles, picked, precision=highest)
    partial_value = jnp.einsum("nr,kni->kri", row_hot, products, precision=highest).reshape(
        count_vectors, -1
    )
    own_rows = lax.psum_scatter(partial_value, "col", scatter_dimension=1, tiled=True)
    result = (own_rows, own_rows)
    return result


def multiply_back(left_rows, block_tiles, tables):
    pick_hot, owners_mine, owner_hot, row_hot, rows_local = tables
    count_vectors = left_rows.shape[0]
    block_size = block_tiles.shape[-1]
    segments = left_rows.reshape(count_vectors, -1, block_size)
    picked = segments[:, rows_local]
    products = jnp.einsum("nij,kni->knj", block_tiles, picked, precision=highest)
    outgoing = jnp.einsum("no,knj->okj", owner_hot, products, precision=highest)
    incoming = lax.all_to_all(outgoing, "row", split_axis=0, concat_axis=0, tiled=True)
    returned = jnp.einsum("rt,rkb->ktb", pick_hot, incoming, precision=highest)
    return returned.reshape(count_vectors, -1)


def shards(blocks, block_rows, block_cols, start_basis, targets):
    block_size = blocks.shape[-1]
    block_tiles = blocks.reshape(-1, block_size, block_size)
    rows_local = block_rows.reshape(-1)
    row_count = lax.axis_size("row")
    col_count = lax.axis_size("col")
    own_width = start_basis.shape[1]
    seg_count = own_width // block_size
    total_rows = float(own_width * row_count * col_count)
    count_vectors = start_basis.shape[0]
    pattern = block_cols[:, 0, :]
    me_row = lax.axis_index("row")
    cols_local = lax.dynamic_index_in_dim(pattern, me_row, 0, keepdims=False)
    owners_mine = cols_local // seg_count
    seg_ids = jnp.arange(seg_count, dtype=jnp.int32)
    matched = pattern // seg_count == me_row
    within = pattern % seg_count
    pick_hot = jnp.any(
        matched[:, :, None] & (within[:, :, None] == seg_ids[None, None, :]), axis=1
    ).astype(jnp.float32)
    owner_hot = (owners_mine[:, None] == jnp.arange(row_count, dtype=jnp.int32)[None, :]).astype(
        jnp.float32
    )
    row_hot = (
        rows_local[:, None] == jnp.arange(col_count * seg_count, dtype=jnp.int32)[None, :]
    ).astype(jnp.float32)
    col_hot = (
        cols_local[:, None] == jnp.arange(row_count * seg_count, dtype=jnp.int32)[None, :]
    ).astype(jnp.float32)
    tables = (pick_hot, owners_mine, owner_hot, row_hot, rows_local)
    squared = jnp.sum(block_tiles * block_tiles, axis=1)
    column_terms = jnp.dot(col_hot.T, squared, precision=highest).reshape(-1)
    squares = lax.psum_scatter(column_terms, "row", scatter_dimension=0, tiled=True)
    largest = lax.pmax(jnp.max(squares), ("row", "col"))
    chosen = jnp.sum(
        (targets[None, :] == jnp.arange(count_vectors, dtype=jnp.int32)[:, None]).astype(
            jnp.float32
        ),
        axis=1,
    )
    trial_basis = start_basis
    left_own = start_basis
    lower_image = jnp.zeros((count_vectors, count_vectors), jnp.float32)
    for outer_step in range(OUTER):
        lower_basis = basis_factor(trial_basis, total_rows)
        right_now = lower_solve(lower_basis, trial_basis)
        image_own, image_rows = multiply(right_now, block_tiles, tables)
        gram_image = lax.psum(gram_local(image_own), ("row", "col"))
        lower_image = jnp.linalg.cholesky(gram_image / total_rows)
        left_own = lower_solve(lower_image, image_own)
        left_rows = lax.all_gather(left_own, "col", axis=1, tiled=True)
        back_own = multiply_back(left_rows, block_tiles, tables)
        residual = back_own - jnp.dot(lower_image.T, right_now, precision=highest)
        shifts = jnp.sum(lower_image * lower_image, axis=1) + largest
        correction = residual / shifts[:, None]
        for inner_step in range(1, INNER):
            coupling = (
                lax.psum(
                    jnp.dot(right_now, (squares[None, :] * correction).T, precision=highest),
                    ("row", "col"),
                )
                / total_rows
            )
            correction = (
                residual
                + squares[None, :] * correction
                - jnp.dot(coupling.T, right_now, precision=highest)
            ) / shifts[:, None]
        trial_basis = right_now + chosen[:, None] * correction
    lower_basis = basis_factor(trial_basis, total_rows)
    return (lower_solve(lower_basis, trial_basis), left_own, lower_image.T)


def solution(mesh):
    in_specs = (
        P("row", "col", None, None, None),
        P("row", "col", None),
        P(None, "col", None),
        P(None, ("row", "col")),
        P(),
    )
    out_specs = (P(None, ("row", "col")), P(None, ("row", "col")), P())
    return jax.shard_map(shards, mesh=mesh, in_specs=in_specs, out_specs=out_specs, check_vma=False)
```

profile of v0, /device:TPU:0, one launch (start us, length us, event | category | flops | bytes accessed | tf_op | source)
XLA Modules:
  0.0 756.0 jit_solution(7076702651899851333)
XLA Ops:
  8.0 0.9 add_select_fusion
  8.9 0.7 fusion.97
  9.9 42.1 %psum.77 = f32[32,32]{0,1:T(8,128)S(1)} all-reduce(f32[32,32]{0,1:T(8,128)S(1)} %fusion.142), channel_id=1, replica_groups=mesh['row'=16,'col'=2] {'row','col'}, use_global_device_ids=true, to_apply=%region_0.1 | all-reduce | flops 1024 | bytes 8192 | tf_op jit(solution)/shard_map/psum | solution.py:20
  52.0 2.9 cholesky.89
  56.3 2.4 custom-call.9
  59.7 0.8 copy.122
  60.5 5.4 all-to-all-start
  67.3 7.6 %all-to-all-done = f32[16,32,128]{2,1,0:T(8,128)S(1)} async-done(((f32[16,32,128]{2,1,0:T(8,128)}), f32[16,32,128]{2,1,0:T(8,128)S(1)}, u32[]{:S(2)}, u32[]{:S(2)}) %all-to-all-start) | async-done | bytes 262176 | tf_op jit(solution)/shard_map/all_to_all | solution.py:30
  75.0 1.4 gather_fusion
  76.4 5.2 fusion.9
  81.6 0.7 fusion.43
  82.4 0.8 copy.198
  83.5 5.5 reduce-scatter.3.cloned.1.call-done
  89.0 1.2 fusion.143
  90.2 40.5 %psum.78 = f32[32,32]{0,1:T(8,128)S(1)} all-reduce(f32[32,32]{0,1:T(8,128)S(1)} %fusion.143), channel_id=1, replica_groups=mesh['row'=16,'col'=2] {'row','col'}, use_global_device_ids=true, to_apply=%region_6.9 | all-reduce | flops 1024 | bytes 8192 | tf_op jit(solution)/shard_map/psum | solution.py:101
  130.8 2.9 cholesky.100
  134.4 0.8 multiply_reduce_fusion.1
  135.2 2.4 custom-call.10
  137.6 1.2 fusion.69
  138.9 2.2 all_gather.6
  141.1 1.4 gather_fusion.1
  142.5 3.5 fusion.12
  146.0 0.7 fusion.41
  146.7 0.8 copy.128
  147.5 5.4 all-to-all-start.1
  153.0 1.0 convolution_bitcast_fusion
  155.4 108.3 %all-reduce.3.cloned.1.call-done = f32[16384]{0:T(1024)} async-done(((f32[16384]{0:T(1024)}), f32[16384]{0:T(1024)}) %all-reduce.3.cloned.1.call-update) | async-done | bytes 65552
  263.7 1.3 fusion.140
  265.0 39.7 %pmax.7 = f32[]{:T(128)} all-reduce(f32[]{:T(128)} %get-tuple-element.23), channel_id=1, replica_groups=mesh['row'=16,'col'=2] {'row','col'}, use_global_device_ids=true, to_apply=%region_11.14 | all-reduce | flops 1 | bytes 8 | tf_op jit(solution)/shard_map/pmax | solution.py:87
  305.7 1.0 convolution_subtract_fusion.7
  307.0 39.9 %psum.79 = f32[32,32]{0,1:T(8,128)S(1)} all-reduce(f32[32,32]{0,1:T(8,128)S(1)} %fusion.49), channel_id=1, replica_groups=mesh['row'=16,'col'=2] {'row','col'}, use_global_device_ids=true, to_apply=%region_12.15 | all-reduce | flops 1024 | bytes 8192 | tf_op jit(solution)/shard_map/psum | solution.py:111
  347.5 40.4 %psum.80 = f32[32,32]{0,1:T(8,128)S(1)} all-reduce(f32[32,32]{0,1:T(8,128)S(1)} %fusion.144), channel_id=1, replica_groups=mesh['row'=16,'col'=2] {'row','col'}, use_global_device_ids=true, to_apply=%region_13.16 | all-reduce | flops 1024 | bytes 8192 | tf_op jit(solution)/shard_map/psum | solution.py:111
  388.4 39.8 %psum.81 = f32[32,32]{0,1:T(8,128)S(1)} all-reduce(f32[32,32]{0,1:T(8,128)S(1)} %fusion.145), channel_id=1, replica_groups=mesh['row'=16,'col'=2] {'row','col'}, use_global_device_ids=true, to_apply=%region_14.17 | all-reduce | flops 1024 | bytes 8192 | tf_op jit(solution)/shard_map/psum | solution.py:111
  428.8 40.3 %psum.82 = f32[32,32]{0,1:T(8,128)S(1)} all-reduce(f32[32,32]{0,1:T(8,128)S(1)} %fusion.146), channel_id=1, replica_groups=mesh['row'=16,'col'=2] {'row','col'}, use_global_device_ids=true, to_apply=%region_15.18 | all-reduce | flops 1024 | bytes 8192 | tf_op jit(solution)/shard_map/psum | solution.py:20
  469.2 2.9 cholesky.111
  473.4 2.4 custom-call.11
  476.6 13.9 %all_to_all.20 = f32[16,32,128]{2,1,0:T(8,128)S(1)} all-to-all(f32[16,32,128]{2,1,0:T(8,128)S(1)} %copy.137), channel_id=1, replica_groups=mesh['row'=16,'col'=2] {'row'}, dimensions={0} | all-to-all | bytes 524288 | tf_op jit(solution)/shard_map/all_to_all | solution.py:30
  490.5 1.4 gather_fusion.2
  491.9 5.2 fusion.15
  497.2 0.7 fusion.39
  497.9 0.8 copy.197
  498.7 5.8 reduce-scatter.5.cloned.1.call-done
  504.5 1.2 fusion.147
  505.8 40.5 %psum.83 = f32[32,32]{0,1:T(8,128)S(1)} all-reduce(f32[32,32]{0,1:T(8,128)S(1)} %fusion.147), channel_id=1, replica_groups=mesh['row'=16,'col'=2] {'row','col'}, use_global_device_ids=true, to_apply=%region_17.20 | all-reduce | flops 1024 | bytes 8192 | tf_op jit(solution)/shard_map/psum | solution.py:101
  546.4 2.9 cholesky.122
  550.0 0.7 fusion.120
  550.7 2.4 custom-call.12
  553.2 1.2 fusion.63
  554.4 2.0 all_gather.7
  556.4 1.4 gather_fusion.3
  557.9 3.4 fusion.18
  561.3 0.7 fusion.37
  562.0 0.8 copy.143
  562.8 5.4 all-to-all-start.3
  568.3 0.7 copy.151
  569.6 8.8 %all-to-all-done.3 = f32[16,32,128]{2,1,0:T(8,128)S(1)} async-done(((f32[16,32,128]{2,1,0:T(8,128)}), f32[16,32,128]{2,1,0:T(8,128)S(1)}, u32[]{:S(2)}, u32[]{:S(2)}) %all-to-all-start.3) | async-done | bytes 262176 | tf_op jit(solution)/shard_map/all_to_all | solution.py:49
  578.8 0.9 convolution_subtract_fusion.3
  580.1 38.9 %psum.84 = f32[32,32]{0,1:T(8,128)S(1)} all-reduce(f32[32,32]{0,1:T(8,128)S(1)} %fusion.50), channel_id=1, replica_groups=mesh['row'=16,'col'=2] {'row','col'}, use_global_device_ids=true, to_apply=%region_19.22 | all-reduce | flops 1024 | bytes 8192 | tf_op jit(solution)/shard_map/psum | solution.py:111
  619.5 39.9 %psum.85 = f32[32,32]{0,1:T(8,128)S(1)} all-reduce(f32[32,32]{0,1:T(8,128)S(1)} %fusion.148), channel_id=1, replica_groups=mesh['row'=16,'col'=2] {'row','col'}, use_global_device_ids=true, to_apply=%region_20.23 | all-reduce | flops 1024 | bytes 8192 | tf_op jit(solution)/shard_map/psum | solution.py:111
  659.9 40.5 %psum.86 = f32[32,32]{0,1:T(8,128)S(1)} all-reduce(f32[32,32]{0,1:T(8,128)S(1)} %fusion.149), channel_id=1, replica_groups=mesh['row'=16,'col'=2] {'row','col'}, use_global_device_ids=true, to_apply=%region_21.24 | all-reduce | flops 1024 | bytes 8192 | tf_op jit(solution)/shard_map/psum | solution.py:111
  700.9 39.9 %psum.87 = f32[32,32]{0,1:T(8,128)S(1)} all-reduce(f32[32,32]{0,1:T(8,128)S(1)} %fusion.150), channel_id=1, replica_groups=mesh['row'=16,'col'=2] {'row','col'}, use_global_device_ids=true, to_apply=%region_22.25 | all-reduce | flops 1024 | bytes 8192 | tf_op jit(solution)/shard_map/psum | solution.py:20
  740.9 2.9 cholesky.133
  745.1 2.4 custom-call.13
  747.6 1.0 fusion.60
  (84 shorter events, 16.0 us)
Async XLA Ops:
  8.0 1.6 copy-start
  8.0 68.4 %copy-start.1 = (f32[1,1,40,128,128]{4,3,2,1,0:T(8,128)S(1)}, f32[1,1,40,128,128]{4,3,2,1,0:T(8,128)}, u32[]{:S(2)}) copy-start(f32[1,1,40,128,128]{4,3,2,1,0:T(8,128)} %param.8) | copy-start | bytes 7864324
  60.5 14.5 %all-to-all-start = ((f32[16,32,128]{2,1,0:T(8,128)}), f32[16,32,128]{2,1,0:T(8,128)S(1)}, u32[]{:S(2)}, u32[]{:S(2)}) async-start(f32[16,32,128]{2,1,0:T(8,128)} %copy.122), calls=%async_computation | async-start | bytes 524288 | tf_op jit(solution)/shard_map/all_to_all | solution.py:30
  65.9 23.1 %reduce-scatter.3.cloned.1.call-start = ((), (), s32[]{:S(2)}) async-start(), calls=%async_computation.6 | async-start | bytes 393216 | tf_op jit(solution)/shard_map/reduce_scatter | solution.py:36
  67.3 14.3 %copy-start.3 = (s32[1,1,40]{2,1,0:T(1,128)S(1)}, s32[1,1,40]{2,1,0:T(1,128)}, u32[]{:S(2)}) copy-start(s32[1,1,40]{2,1,0:T(1,128)} %param.9) | copy-start | bytes 484
  142.5 11.5 %copy-start.5 = (u32[32]{0:T(128)S(1)}, u32[32]{0:T(128)}, u32[]{:S(2)}) copy-start(u32[32]{0:T(128)} %constant.104) | copy-start | bytes 388
  142.5 12.7 %copy-start.4 = (s32[16]{0:T(128)S(1)}, s32[16]{0:T(128)}, u32[]{:S(2)}) copy-start(s32[16]{0:T(128)} %param.12) | copy-start | bytes 196
  147.5 157.9 %all-to-all-start.1 = ((f32[16,32,128]{2,1,0:T(8,128)}), f32[16,32,128]{2,1,0:T(8,128)S(1)}, u32[]{:S(2)}, u32[]{:S(2)}) async-start(f32[16,32,128]{2,1,0:T(8,128)} %copy.128), calls=%async_computation.2 | async-start | bytes 524288 | tf_op jit(solution)/shard_map/all_to_all | solution.py:49
  152.9 110.8 %all-reduce.3.cloned.1.call-start = ((), (), s32[]{:S(2)}) async-start(), calls=%async_computation.8 | async-start | bytes 131072
  154.0 350.6 %reduce-scatter.5.cloned.1.call-start = ((), (), s32[]{:S(2)}) async-start(), calls=%async_computation.7 | async-start | bytes 393216 | tf_op jit(solution)/shard_map/reduce_scatter | solution.py:36
  554.4 6.9 copy-start.2
  562.8 15.6 %all-to-all-start.3 = ((f32[16,32,128]{2,1,0:T(8,128)}), f32[16,32,128]{2,1,0:T(8,128)S(1)}, u32[]{:S(2)}, u32[]{:S(2)}) async-start(f32[16,32,128]{2,1,0:T(8,128)} %copy.143), calls=%async_computation.5 | async-start | bytes 524288 | tf_op jit(solution)/shard_map/all_to_all | solution.py:49
Sparse Core Ops, SparseCore 0:
  83.3 5.6 reduce-scatter.2
  498.8 5.6 reduce-scatter.4
Sparse Core Ops, SparseCore 1:
  159.5 104.2 all-reduce.2
where the time goes:
time: 759 us; the launch traced here: 756 us
  blocking collectives  501 us (66%)
  waiting for transfers between devices  136 us (18%)
  other arithmetic  39.9 us (5%)
  matrix products  34.9 us (5%)
  between operations  16.6 us (2%)
  starting transfers between devices  16.5 us (2%)
  local copies, waits for them, and re-layouts  11.4 us (2%)
    psum x6, blocking collectives, shards(): lax.psum(jnp.dot(right_now, (squares[None, :] * correction).T, precision=...  239 us
    psum x3, blocking collectives, basis_factor(): gram_sum = lax.psum(gram_local(trial_basis), ('row', 'col'))  122 us
    unnamed x4, waiting for transfers between devices  108 us
    psum x2, blocking collectives, shards(): gram_image = lax.psum(gram_local(image_own), ('row', 'col'))  81 us
    pmax x1, blocking collectives, shards(): largest = lax.pmax(jnp.max(squares), ('row', 'col'))  39.7 us
  transfers between devices with their start and end apart: 6, of which 5 were waited for; matrix products, arithmetic and copies ran while one was open for 1% of the time, Pallas kernels for 0%

commit v1 on v0

--- a/solution.py
+++ b/solution.py
@@ -98,7 +98,7 @@
         lower_basis = basis_factor(trial_basis, total_rows)
         right_now = lower_solve(lower_basis, trial_basis)
         image_own, image_rows = multiply(right_now, block_tiles, tables)
-        gram_image = lax.psum(gram_local(image_own), ("row", "col"))
+        gram_image = lax.psum(lax.psum(gram_local(image_own), "col"), "row")
         lower_image = jnp.linalg.cholesky(gram_image / total_rows)
         left_own = lower_solve(lower_image, image_own)
         left_rows = lax.all_gather(left_own, "col", axis=1, tiled=True)

time: 759 us -> 834 us (1.099)
  blocking collectives: 501 us -> 580 us
    psum x2 -> x4, blocking collectives: 81 us -> 161 us  [shards(): gram_image = lax.psum(lax.psum(gram_local(image_own), 'col'), 'row')]
where the time goes in v1:
time: 834 us; the launch traced here: 832 us
  blocking collectives  580 us (70%)
  waiting for transfers between devices  136 us (16%)
  other arithmetic  39.9 us (5%)
  matrix products  34.9 us (4%)
  between operations  16.6 us (2%)
  starting transfers between devices  12.8 us (2%)
  local copies, waits for them, and re-layouts  11.4 us (1%)
    psum x6, blocking collectives, shards(): lax.psum(jnp.dot(right_now, (squares[None, :] * correction).T, precision=...  239 us
    psum x4, blocking collectives, shards(): gram_image = lax.psum(lax.psum(gram_local(image_own), 'col'), 'row')  161 us
    psum x3, blocking collectives, basis_factor(): gram_sum = lax.psum(gram_local(trial_basis), ('row', 'col'))  122 us
    unnamed x4, waiting for transfers between devices  108 us
    pmax x1, blocking collectives, shards(): largest = lax.pmax(jnp.max(squares), ('row', 'col'))  39.7 us
  transfers between devices with their start and end apart: 6, of which 5 were waited for; matrix products, arithmetic and copies ran while one was open for 1% of the time, Pallas kernels for 0%

profile of v1, /device:TPU:0, one launch (start us, length us, event | category | flops | bytes accessed | tf_op | source)
XLA Modules:
  0.0 831.9 jit_solution(4133370503937087205)
XLA Ops:
  8.0 0.9 add_select_fusion
  8.9 0.7 fusion.97
  9.9 42.1 %psum.91 = f32[32,32]{0,1:T(8,128)S(1)} all-reduce(f32[32,32]{0,1:T(8,128)S(1)} %fusion.142), channel_id=1, replica_groups=mesh['row'=16,'col'=2] {'row','col'}, use_global_device_ids=true, to_apply=%region_0.1 | all-reduce | flops 1024 | bytes 8192 | tf_op jit(solution)/shard_map/psum | solution.py:20
  52.0 2.9 cholesky.89
  56.3 2.4 custom-call.9
  59.7 0.8 copy.122
  60.5 5.4 all-to-all-start
  67.3 7.6 all-to-all-done
  75.0 1.4 gather_fusion
  76.4 5.2 fusion.9
  81.6 0.7 fusion.43
  82.4 0.8 copy.198
  83.5 5.5 reduce-scatter.3.cloned.1.call-done
  89.0 1.2 fusion.143
  90.2 3.4 psum.92
  93.6 77.1 %psum.93 = f32[32,32]{0,1:T(8,128)S(1)} all-reduce(f32[32,32]{0,1:T(8,128)S(1)} %psum.92), channel_id=1, replica_groups=mesh['row'=16,'col'=2] {'row'}, use_global_device_ids=true, to_apply=%region_7.10 | all-reduce | flops 1024 | bytes 8192 | tf_op jit(solution)/shard_map/psum | solution.py:101
  170.8 2.9 cholesky.100
  174.4 0.8 multiply_reduce_fusion.1
  175.1 2.4 custom-call.10
  177.6 1.2 fusion.69
  178.8 2.0 all_gather.6
  180.9 1.4 gather_fusion.1
  182.3 3.5 fusion.12
  185.8 0.7 fusion.41
  186.5 0.8 copy.128
  187.2 3.5 all-to-all-start.1
  191.0 1.0 convolution_bitcast_fusion
  193.4 108.1 %all-reduce.3.cloned.1.call-done = f32[16384]{0:T(1024)} async-done(((f32[16384]{0:T(1024)}), f32[16384]{0:T(1024)}) %all-reduce.3.cloned.1.call-update) | async-done | bytes 65552
  301.5 1.3 fusion.140
  302.8 39.7 %pmax.7 = f32[]{:T(128)} all-reduce(f32[]{:T(128)} %get-tuple-element.23), channel_id=1, replica_groups=mesh['row'=16,'col'=2] {'row','col'}, use_global_device_ids=true, to_apply=%region_12.15 | all-reduce | flops 1 | bytes 8 | tf_op jit(solution)/shard_map/pmax | solution.py:87
  343.6 1.0 convolution_subtract_fusion.7
  344.9 39.9 %psum.94 = f32[32,32]{0,1:T(8,128)S(1)} all-reduce(f32[32,32]{0,1:T(8,128)S(1)} %fusion.49), channel_id=1, replica_groups=mesh['row'=16,'col'=2] {'row','col'}, use_global_device_ids=true, to_apply=%region_13.16 | all-reduce | flops 1024 | bytes 8192 | tf_op jit(solution)/shard_map/psum | solution.py:111
  385.4 40.4 %psum.95 = f32[32,32]{0,1:T(8,128)S(1)} all-reduce(f32[32,32]{0,1:T(8,128)S(1)} %fusion.144), channel_id=1, replica_groups=mesh['row'=16,'col'=2] {'row','col'}, use_global_device_ids=true, to_apply=%region_14.17 | all-reduce | flops 1024 | bytes 8192 | tf_op jit(solution)/shard_map/psum | solution.py:111
  426.3 39.8 %psum.96 = f32[32,32]{0,1:T(8,128)S(1)} all-reduce(f32[32,32]{0,1:T(8,128)S(1)} %fusion.145), channel_id=1, replica_groups=mesh['row'=16,'col'=2] {'row','col'}, use_global_device_ids=true, to_apply=%region_15.18 | all-reduce | flops 1024 | bytes 8192 | tf_op jit(solution)/shard_map/psum | solution.py:111
  466.6 40.3 %psum.97 = f32[32,32]{0,1:T(8,128)S(1)} all-reduce(f32[32,32]{0,1:T(8,128)S(1)} %fusion.146), channel_id=1, replica_groups=mesh['row'=16,'col'=2] {'row','col'}, use_global_device_ids=true, to_apply=%region_16.19 | all-reduce | flops 1024 | bytes 8192 | tf_op jit(solution)/shard_map/psum | solution.py:20
  507.0 2.9 cholesky.111
  511.3 2.4 custom-call.11
  514.5 13.9 %all_to_all.20 = f32[16,32,128]{2,1,0:T(8,128)S(1)} all-to-all(f32[16,32,128]{2,1,0:T(8,128)S(1)} %copy.137), channel_id=1, replica_groups=mesh['row'=16,'col'=2] {'row'}, dimensions={0} | all-to-all | bytes 524288 | tf_op jit(solution)/shard_map/all_to_all | solution.py:30
  528.3 1.4 gather_fusion.2
  529.8 5.2 fusion.15
  535.0 0.7 fusion.39
  535.7 0.8 copy.197
  536.5 5.8 reduce-scatter.5.cloned.1.call-done
  542.4 1.2 fusion.147
  543.6 3.4 psum.98
  547.0 77.1 %psum.99 = f32[32,32]{0,1:T(8,128)S(1)} all-reduce(f32[32,32]{0,1:T(8,128)S(1)} %psum.98), channel_id=1, replica_groups=mesh['row'=16,'col'=2] {'row'}, use_global_device_ids=true, to_apply=%region_19.22 | all-reduce | flops 1024 | bytes 8192 | tf_op jit(solution)/shard_map/psum | solution.py:101
  624.2 2.9 cholesky.122
  627.8 0.7 fusion.120
  628.5 2.4 custom-call.12
  630.9 1.2 fusion.63
  632.2 2.0 all_gather.7
  634.2 1.4 gather_fusion.3
  635.7 3.4 fusion.18
  639.8 0.8 copy.143
  640.6 3.5 all-to-all-start.3
  645.5 9.1 %all-to-all-done.3 = f32[16,32,128]{2,1,0:T(8,128)S(1)} async-done(((f32[16,32,128]{2,1,0:T(8,128)}), f32[16,32,128]{2,1,0:T(8,128)S(1)}, u32[]{:S(2)}, u32[]{:S(2)}) %all-to-all-start.3) | async-done | bytes 262176 | tf_op jit(solution)/shard_map/all_to_all | solution.py:49
  654.9 0.9 convolution_subtract_fusion.3
  656.2 38.9 %psum.100 = f32[32,32]{0,1:T(8,128)S(1)} all-reduce(f32[32,32]{0,1:T(8,128)S(1)} %fusion.50), channel_id=1, replica_groups=mesh['row'=16,'col'=2] {'row','col'}, use_global_device_ids=true, to_apply=%region_21.24 | all-reduce | flops 1024 | bytes 8192 | tf_op jit(solution)/shard_map/psum | solution.py:111
  695.5 39.9 %psum.101 = f32[32,32]{0,1:T(8,128)S(1)} all-reduce(f32[32,32]{0,1:T(8,128)S(1)} %fusion.148), channel_id=1, replica_groups=mesh['row'=16,'col'=2] {'row','col'}, use_global_device_ids=true, to_apply=%region_22.25 | all-reduce | flops 1024 | bytes 8192 | tf_op jit(solution)/shard_map/psum | solution.py:111
  736.0 40.2 %psum.102 = f32[32,32]{0,1:T(8,128)S(1)} all-reduce(f32[32,32]{0,1:T(8,128)S(1)} %fusion.149), channel_id=1, replica_groups=mesh['row'=16,'col'=2] {'row','col'}, use_global_device_ids=true, to_apply=%region_23.26 | all-reduce | flops 1024 | bytes 8192 | tf_op jit(solution)/shard_map/psum | solution.py:111
  776.8 39.9 %psum.103 = f32[32,32]{0,1:T(8,128)S(1)} all-reduce(f32[32,32]{0,1:T(8,128)S(1)} %fusion.150), channel_id=1, replica_groups=mesh['row'=16,'col'=2] {'row','col'}, use_global_device_ids=true, to_apply=%region_24.27 | all-reduce | flops 1024 | bytes 8192 | tf_op jit(solution)/shard_map/psum | solution.py:20
  816.7 2.9 cholesky.133
  821.0 2.4 custom-call.13
  823.4 1.0 fusion.60
  (86 shorter events, 17.5 us)
Async XLA Ops:
  8.0 1.6 copy-start
  8.0 68.4 %copy-start.1 = (f32[1,1,40,128,128]{4,3,2,1,0:T(8,128)S(1)}, f32[1,1,40,128,128]{4,3,2,1,0:T(8,128)}, u32[]{:S(2)}) copy-start(f32[1,1,40,128,128]{4,3,2,1,0:T(8,128)} %param.8) | copy-start | bytes 7864324
  60.5 14.5 %all-to-all-start = ((f32[16,32,128]{2,1,0:T(8,128)}), f32[16,32,128]{2,1,0:T(8,128)S(1)}, u32[]{:S(2)}, u32[]{:S(2)}) async-start(f32[16,32,128]{2,1,0:T(8,128)} %copy.122), calls=%async_computation | async-start | bytes 524288 | tf_op jit(solution)/shard_map/all_to_all | solution.py:30
  65.9 23.1 %reduce-scatter.3.cloned.1.call-start = ((), (), s32[]{:S(2)}) async-start(), calls=%async_computation.6 | async-start | bytes 393216 | tf_op jit(solution)/shard_map/reduce_scatter | solution.py:36
  67.3 14.3 %copy-start.3 = (s32[1,1,40]{2,1,0:T(1,128)S(1)}, s32[1,1,40]{2,1,0:T(1,128)}, u32[]{:S(2)}) copy-start(s32[1,1,40]{2,1,0:T(1,128)} %param.9) | copy-start | bytes 484
  182.3 9.8 %copy-start.5 = (u32[32]{0:T(128)S(1)}, u32[32]{0:T(128)}, u32[]{:S(2)}) copy-start(u32[32]{0:T(128)} %constant.104) | copy-start | bytes 388
  182.3 11.0 %copy-start.4 = (s32[16]{0:T(128)S(1)}, s32[16]{0:T(128)}, u32[]{:S(2)}) copy-start(s32[16]{0:T(128)} %param.12) | copy-start | bytes 196
  187.2 156.0 %all-to-all-start.1 = ((f32[16,32,128]{2,1,0:T(8,128)}), f32[16,32,128]{2,1,0:T(8,128)S(1)}, u32[]{:S(2)}, u32[]{:S(2)}) async-start(f32[16,32,128]{2,1,0:T(8,128)} %copy.128), calls=%async_computation.2 | async-start | bytes 524288 | tf_op jit(solution)/shard_map/all_to_all | solution.py:49
  190.8 110.8 %all-reduce.3.cloned.1.call-start = ((), (), s32[]{:S(2)}) async-start(), calls=%async_computation.8 | async-start | bytes 131072
  192.0 350.4 %reduce-scatter.5.cloned.1.call-start = ((), (), s32[]{:S(2)}) async-start(), calls=%async_computation.7 | async-start | bytes 393216 | tf_op jit(solution)/shard_map/reduce_scatter | solution.py:36
  632.2 6.9 copy-start.2
  640.6 13.9 %all-to-all-start.3 = ((f32[16,32,128]{2,1,0:T(8,128)}), f32[16,32,128]{2,1,0:T(8,128)S(1)}, u32[]{:S(2)}, u32[]{:S(2)}) async-start(f32[16,32,128]{2,1,0:T(8,128)} %copy.143), calls=%async_computation.5 | async-start | bytes 524288 | tf_op jit(solution)/shard_map/all_to_all | solution.py:49
Sparse Core Ops, SparseCore 0:
  83.3 5.6 reduce-scatter.2
  536.7 5.6 reduce-scatter.4
Sparse Core Ops, SparseCore 1:
  197.3 104.2 all-reduce.2
